TPU v7x, 32 devices: a whole 2x2x4 slice. The times are simulated.
32 devices in a mesh: cone: 4 (over y, x), con: 8 (over z, core).
Axes of the slice: x: 2, y: 2, z: 4, core: 2. Of those that a mesh axis runs over, the one named last changes fastest.
Arguments:
- vectors: bfloat16 [4, 8192, 1024], P('cone', 'con'), may hold values from -0.1875 to 0.1875
- primal: bfloat16 [4, 1024, 1024], P('cone'), may hold values from -8 to 8, as said below
- dual_inverse: bfloat16 [4, 1024, 1024], P('cone'), may hold values from -8 to 8, as said below
- touches: int32 [4, 8], P('cone'), may hold values from 0 to 1, as said below
Outputs:
- slab: float32 [2048, 8192], P('cone', 'con')
Inputs may be any that keep to these rules, and one draw needn't show every extreme that they name: `primal`: symmetric and positive definite in every cone. `dual_inverse`: symmetric and positive definite in every cone. Every constraint block touches at least one cone.
All inputs are finite; a program needn't handle non-finite values.
Results may differ from a plain program's by a relative error of at most 0.00079.
Values may be sent and summed in bfloat16 or wider, within the bound.
No kernel may reach another device: no remote copies, remote signals or barrier semaphores. Data moves between devices by JAX's collectives and lax.ppermute only.
A program may use at most 128 MiB of HBM per device.

v0:
```python
import jax
import jax.numpy as jnp
from jax import lax
from jax.sharding import PartitionSpec as P

PANEL = 512


def broadcast(value, axis, source):
    kept = jnp.where(lax.axis_index(axis) == source, value, 0).astype(value.dtype)
    return lax.psum(kept, axis)


def shards(vectors, primal, dual_inverse, touches):
    con_count = lax.axis_size("con")
    cone_count = lax.axis_size("cone")
    con_place = lax.axis_index("con")
    cone_place = lax.axis_index("cone")
    per_block = vectors.shape[1]
    row_dev = PANEL * cone_count // con_count
    owners = con_count // cone_count
    touched = touches[0]
    own_flag = lax.dynamic_index_in_dim(touched, con_place, 0, keepdims=False)
    own_vectors = vectors[0] * own_flag.astype(jnp.bfloat16)
    primal_block = primal[0]
    dual_block = dual_inverse[0]
    row_vectors = lax.all_gather(own_vectors[:row_dev], "con", axis=0, tiled=True)
    row_primal = jnp.dot(row_vectors, primal_block, preferred_element_type=jnp.float32).astype(
        jnp.bfloat16
    )
    row_dual = jnp.dot(row_vectors, dual_block, preferred_element_type=jnp.float32).astype(
        jnp.bfloat16
    )
    contract = (((1,), (1,)), ((), ()))
    gram_primal = lax.dot_general(
        row_primal, own_vectors, contract, preferred_element_type=jnp.float32
    )
    gram_dual = lax.dot_general(row_dual, own_vectors, contract, preferred_element_type=jnp.float32)
    schur_slab = lax.psum_scatter(gram_primal * gram_dual, "cone", scatter_dimension=0, tiled=True)
    panel_block = broadcast(schur_slab, "cone", 0)
    leading_columns = panel_block[:, :row_dev]
    gathered = lax.all_gather(leading_columns, "con", axis=1, tiled=True)
    pivot_source = gathered[:, :PANEL]
    block_source = lax.dynamic_slice_in_dim(gathered, cone_place * PANEL, PANEL, 1)
    pivot_matrix = (pivot_source + pivot_source.T) * 0.5
    lower_factor = jnp.linalg.cholesky(pivot_matrix)
    combined = jnp.concatenate([panel_block, block_source], axis=1)
    solved = jax.scipy.linalg.solve_triangular(lower_factor, combined, lower=True)
    factor_rows = solved[:, :per_block]
    row_factor = solved[:, per_block:]
    updated = schur_slab - jnp.einsum(
        "kr,kc->rc", row_factor, factor_rows, precision=lax.Precision.HIGHEST
    )
    local_columns = jnp.arange(per_block, dtype=jnp.int32)
    pivot_column = (con_place < owners) & (local_columns < row_dev)
    remaining = jnp.where(pivot_column[None, :], 0.0, updated)
    return jnp.where(cone_place == 0, factor_rows, remaining)


def solution(mesh):
    in_specs = (
        P("cone", "con", None),
        P("cone", None, None),
        P("cone", None, None),
        P("cone", None),
    )
    out_specs = P("cone", "con")
    return jax.shard_map(shards, mesh=mesh, in_specs=in_specs, out_specs=out_specs, check_vma=False)
```

profile of v0, /device:TPU:0, one launch (start us, length us, event | category | flops | bytes accessed | tf_op | source)
XLA Modules:
  0.0 488.2 jit_solution(6037763311798876884)
XLA Ops:
  6.5 1.4 fusion.61
  7.9 2.4 broadcast_multiply_fusion
  10.3 1.3 copy-done.7
  11.6 0.8 slice.149
  12.5 49.7 %all-gather.6.cloned.1.call-done = bf16[1,2048,1024]{2,1,0:T(8,128)(2,1)} async-done(((bf16[1,256,1024]{2,1,0:T(8,128)(2,1)}), bf16[1,2048,1024]{2,1,0:T(8,128)(2,1)}) %all-gather.6.cloned.1.call-update) | async-done | bytes 4194320 | tf_op jit(solution)/shard_map/all_gather | solution.py:27
  62.2 7.1 %fusion.2 = bf16[2048,1024]{1,0:T(8,128)(2,1)S(1)} fusion(bf16[1,2048,1024]{2,1,0:T(8,128)(2,1)} %all-gather.6.cloned.1.call-done, bf16[1,1024,1024]{2,1,0:T(8,128)(2,1)S(1)} %copy-done), kind=kOutput, calls=%fused_computation.8 | convolution fusion | flops 4294967296 | bytes 10485760 | tf_op jit(solution)/shard_map/dot_general | solution.py:28
  69.3 4.6 fusion.5
  73.9 4.7 fusion
  78.7 6.8 %convolution_multiply_fusion = f32[2048,1024]{0,1:T(8,128)} fusion(f32[2048,1024]{0,1:T(8,128)S(1)} %fusion.5, bf16[2048,1024]{1,0:T(8,128)(2,1)S(1)} %fusion, bf16[1,1024,1024]{2,1,0:T(8,128)(2,1)S(1)} %copy-done.8), kind=kOutput, calls=%fused_computation.5 | convolution fusion | flops 4297064448 | bytes 23068672 | tf_op jit(solution)/shard_map/dot_general | solution.py:38
  85.5 85.2 %reduce-scatter.2.cloned.1.call-done = f32[512,1024]{0,1:T(8,128)} async-done(((f32[2048,1024]{0,1:T(8,128)}), f32[512,1024]{0,1:T(8,128)}) %reduce-scatter.2.cloned.1.call-update) | async-done | bytes 2097168 | tf_op jit(solution)/shard_map/reduce_scatter | solution.py:39
  170.7 3.1 broadcast_select_fusion
  174.1 69.2 %all-reduce.3.cloned.1.call-done = f32[512,1024]{0,1:T(8,128)} async-done(((f32[512,1024]{0,1:T(8,128)}), f32[512,1024]{0,1:T(8,128)}) %all-reduce.3.cloned.1.call-update) | async-done | bytes 2097168 | tf_op jit(solution)/shard_map/psum | solution.py:11
  243.3 1.9 slice.150
  245.3 47.0 %all-gather.4.cloned.1.call-done = f32[512,2048]{0,1:T(8,128)} async-done(((f32[512,256]{0,1:T(8,128)}), f32[512,2048]{0,1:T(8,128)}) %all-gather.4.cloned.1.call-update) | async-done | bytes 4194320 | tf_op jit(solution)/shard_map/all_gather | solution.py:42
  292.3 1.7 fusion.60
  294.0 0.3 copy.7
  294.3 1.4 fusion.31
  295.8 0.3 copy.8
  296.1 0.2 fusion.30
  296.4 1.0 copy-done.9
  297.4 11.7 %cholesky.104 = f32[128,128]{1,0:T(8,128)S(1)} custom-call(f32[128,128]{1,0:T(8,128)S(1)} %cholesky.266), custom_call_target="Cholesky" | custom-call | tf_op jit(solution)/shard_map/jit(cholesky)/cholesky | solution.py:46
  309.1 1.1 cholesky.224
  310.2 9.8 %custom-call.31 = f32[1,128,128]{1,2,0:T(8,128)S(1)} custom-call(f32[1,128,128]{2,1,0:T(8,128)S(1)} %get-tuple-element.34), custom_call_target="InvertDiagBlocksLowerTriangular" | custom-call | tf_op jit(solution)/shard_map/jit(cholesky)/cholesky | solution.py:46
  320.0 1.9 constant_dynamic-update-slice_fusion.3
  321.9 1.2 convolution_subtract_fusion.3
  323.2 11.7 %cholesky.217 = f32[128,128]{1,0:T(8,128)S(1)} custom-call(f32[128,128]{1,0:T(8,128)S(1)} %cholesky.270), custom_call_target="Cholesky" | custom-call | tf_op jit(solution)/shard_map/jit(cholesky)/cholesky | solution.py:46
  334.9 0.6 select_reduce_fusion.2
  335.6 10.2 %custom-call.32 = f32[1,128,128]{1,2,0:T(8,128)S(1)} custom-call(f32[1,128,128]{2,1,0:T(8,128)S(1)} %get-tuple-element.31), custom_call_target="InvertDiagBlocksLowerTriangular" | custom-call | tf_op jit(solution)/shard_map/jit(cholesky)/cholesky | solution.py:46
  345.8 0.9 convolution_dynamic-update-slice_fusion
  346.7 1.6 convolution_subtract_fusion.4
  348.3 11.7 %cholesky.238 = f32[128,128]{1,0:T(8,128)S(1)} custom-call(f32[128,128]{1,0:T(8,128)S(1)} %cholesky.275), custom_call_target="Cholesky" | custom-call | tf_op jit(solution)/shard_map/jit(cholesky)/cholesky | solution.py:46
  360.0 0.6 select_reduce_fusion.1
  360.6 0.7 compare_reduce_fusion.1
  361.3 9.8 %custom-call.33 = f32[1,128,128]{1,2,0:T(8,128)S(1)} custom-call(f32[1,128,128]{2,1,0:T(8,128)S(1)} %get-tuple-element.28), custom_call_target="InvertDiagBlocksLowerTriangular" | custom-call | tf_op jit(solution)/shard_map/jit(cholesky)/cholesky | solution.py:46
  371.1 0.8 convolution_dynamic-update-slice_fusion.1
  372.0 1.4 convolution_subtract_fusion.5
  373.4 11.9 %cholesky.255 = f32[128,128]{1,0:T(8,128)S(1)} custom-call(f32[128,128]{1,0:T(8,128)S(1)} %convolution_subtract_fusion.5), custom_call_target="Cholesky" | custom-call | tf_op jit(solution)/shard_map/jit(cholesky)/cholesky | solution.py:46
  385.3 0.6 select_reduce_fusion
  385.9 0.7 compare_reduce_fusion
  386.6 0.7 compare_reduce_fusion.2
  389.8 2.3 select_select_fusion.1
  392.1 14.0 %while.1 = (s32[]{:T(128)}, f32[512,512]{1,0:T(8,128)}, s32[4,2]{0,1:T(2,128)S(1)}, f32[4,128,128]{2,1,0:T(8,128)}, s32[]{:T(128)}) while((s32[]{:T(128)}, f32[512,512]{1,0:T(8,128)}, s32[4,2]{0,1:T(2,128)S(1)}, f32[4,128,128]{2,1,0:T(8,128)}, s32[]{:T(128)}) %tuple.28), condition=%wide.while_cond, body=%wide.while_body.sunk | while | flops 2 | bytes 132705 | solution.py:48
  392.2 0.6 fusion.70
  392.7 2.9 bitcast_dynamic-update-slice_fusion.2
  395.7 0.6 fusion.70
  396.3 2.9 bitcast_dynamic-update-slice_fusion.2
  399.2 0.6 fusion.70
  399.8 2.9 bitcast_dynamic-update-slice_fusion.2
  402.7 0.6 fusion.70
  403.3 2.8 bitcast_dynamic-update-slice_fusion.2
  406.1 40.1 %custom-call.34 = f32[4,128,128]{1,2,0:T(8,128)S(1)} custom-call(f32[4,128,128]{2,1,0:T(8,128)} %get-tuple-element.12), custom_call_target="InvertDiagBlocksLowerTriangular" | custom-call | tf_op jit(solution)/shard_map/jit(_solve_triangular)/triangular_solve | solution.py:48
  446.3 1.8 fusion.34
  448.0 2.3 copy.9
  450.3 2.6 convolution_subtract_fusion.2
  452.9 1.7 fusion.48
  454.7 2.3 copy.10
  456.9 4.1 convolution_subtract_fusion
  461.0 1.8 fusion.46
  462.8 2.3 copy.11
  465.1 6.1 %convolution_subtract_fusion.1 = f32[128,1536]{0,1:T(8,128)S(1)} fusion(f32[128,1536]{1,0:T(8,128)} %fusion.46, f32[128,1536]{1,0:T(8,128)} %fusion.48, f32[128,1536]{1,0:T(8,128)} %fusion.34, f32[512,512]{0,1:T(8,128)S(1)} %get-tuple-element.24, f32[512,1024]{0,1:T(8,128)S(1)} %copy-done.2, f32[512,512]{1,0:T(8,128)} %get-tuple-element.93), kind=kOutput, calls=%fused_computation.18 | convolution fusion | flops 907542528 | bytes 6488064 | tf_op jit(solution)/shard_map/jit(_solve_triangular)/triangular_solve | solution.py:48
  471.2 0.8 fusion.45
  472.2 1.4 copy-done.3
  473.6 5.0 %select_select_fusion = f32[512,1024]{0,1:T(8,128)} fusion(f32[512,1024]{0,1:T(8,128)S(1)} %copy-done.3, f32[512,1536]{0,1:T(8,128)S(1)} %pad_maximum_fusion, f32[128,1536]{0,1:T(8,128)S(1)} %fusion.45, f32[128,1536]{0,1:T(8,128)S(1)} %copy-done.6, f32[128,1536]{0,1:T(8,128)S(1)} %copy-done.5, f32[128,1536]{0,1:T(8,128)S(1)} %copy-done.4, ...), kind=kOutput, calls=%fused_computation.29 | convolution fusion | flops 3223584768 | bytes 11535361 | tf_op jit(solution)/shard_map/kr,kc->rc/dot_general | solution.py:51
  478.6 2.9 copy.14
  (42 shorter events, 1.0 us)
Async XLA Ops:
  6.5 55.7 %copy-start = (bf16[1,1024,1024]{2,1,0:T(8,128)(2,1)S(1)}, bf16[1,1024,1024]{2,1,0:T(8,128)(2,1)}, u32[]{:S(2)}) copy-start(bf16[1,1024,1024]{2,1,0:T(8,128)(2,1)} %param.5) | copy-start | bytes 6291460
  6.5 55.7 %all-gather.6.cloned.1.call-start = ((), (), s32[]{:S(2)}) async-start(), calls=%async_computation.4 | async-start | bytes 4718592 | tf_op jit(solution)/shard_map/all_gather | solution.py:27
  10.3 1.3 copy-start.7
  12.5 158.2 %reduce-scatter.2.cloned.1.call-start = ((), (), s32[]{:S(2)}) async-start(), calls=%async_computation.1 | async-start | bytes 10485760 | tf_op jit(solution)/shard_map/reduce_scatter | solution.py:39
  62.2 7.1 %copy-start.8 = (bf16[1,1024,1024]{2,1,0:T(8,128)(2,1)S(1)}, bf16[1,1024,1024]{2,1,0:T(8,128)(2,1)}, u32[]{:S(2)}) copy-start(bf16[1,1024,1024]{2,1,0:T(8,128)(2,1)} %copy-done.7) | copy-start | bytes 6291460
  69.3 4.6 copy-start.10
  69.3 4.6 copy-start.11
  85.5 157.9 %all-reduce.3.cloned.1.call-start = ((), (), s32[]{:S(2)}) async-start(), calls=%async_computation.2 | async-start | bytes 4194304 | tf_op jit(solution)/shard_map/psum | solution.py:11
  173.9 118.4 %all-gather.4.cloned.1.call-start = ((), (), s32[]{:S(2)}) async-start(), calls=%async_computation.3 | async-start | bytes 4718592 | tf_op jit(solution)/shard_map/all_gather | solution.py:42
  296.4 1.0 copy-start.9
  346.7 99.6 %copy-start.2 = (f32[512,1024]{0,1:T(8,128)S(1)}, f32[512,1024]{0,1:T(8,128)}, u32[]{:S(2)}) copy-start(f32[512,1024]{0,1:T(8,128)} %all-reduce.3.cloned.1.call-done) | copy-start | bytes 6291460
  465.1 6.9 %copy-start.4 = (f32[128,1536]{0,1:T(8,128)S(1)}, f32[128,1536]{0,1:T(8,128)}, u32[]{:S(2)}) copy-start(f32[128,1536]{0,1:T(8,128)} %copy.9) | copy-start | bytes 2359300
  465.1 6.9 %copy-start.5 = (f32[128,1536]{0,1:T(8,128)S(1)}, f32[128,1536]{0,1:T(8,128)}, u32[]{:S(2)}) copy-start(f32[128,1536]{0,1:T(8,128)} %copy.10) | copy-start | bytes 2359300
  465.1 6.9 %copy-start.6 = (f32[128,1536]{0,1:T(8,128)S(1)}, f32[128,1536]{0,1:T(8,128)}, u32[]{:S(2)}) copy-start(f32[128,1536]{0,1:T(8,128)} %copy.11) | copy-start | bytes 2359300
  472.0 1.6 copy-start.3
  473.6 7.9 %copy-start.1 = (bf16[1,1024,1024]{2,1,0:T(8,128)(2,1)S(1)}, bf16[1,1024,1024]{2,1,0:T(8,128)(2,1)}, u32[]{:S(2)}) copy-start(bf16[1,1024,1024]{2,1,0:T(8,128)(2,1)} %param.5) | copy-start | bytes 6291460
Sparse Core Ops, SparseCore 0:
  12.6 49.5 all-gather.5
  85.6 85.1 reduce-scatter.1
  174.0 69.2 all-reduce.2
  245.4 46.8 all-gather.3
where the time goes:
time: 497 us; the launch traced here: 488 us
  waiting for transfers between devices  251 us (51%)
  other arithmetic  132 us (27%)
  matrix products  54.8 us (11%)
  local copies, waits for them, and re-layouts  33.7 us (7%)
  between operations  16.2 us (3%)
    reduce_scatter x1, waiting for transfers between devices, shards(): lax.psum_scatter(gram_primal * gram_dual, 'cone', scatter_dimension=0, ti...  85.2 us
    another operation x14, other arithmetic, shards(): lower_factor = jnp.linalg.cholesky(pivot_matrix)  80.8 us
    psum x1, waiting for transfers between devices, broadcast(): return lax.psum(kept, axis)  69.2 us
    all_gather x1, waiting for transfers between devices, shards(): lax.all_gather(own_vectors[:row_dev], 'con', axis=0, tiled=True)  49.7 us
    all_gather x1, waiting for transfers between devices, shards(): gathered = lax.all_gather(leading_columns, 'con', axis=1, tiled=True)  47 us
    another operation x4, other arithmetic, shards(): jax.scipy.linalg.solve_triangular(lower_factor, combined, lower=True)  42.7 us
    another operation x7, matrix products, shards(): jax.scipy.linalg.solve_triangular(lower_factor, combined, lower=True)  18.8 us
    another operation x12, local copies, waits for them, and re-layouts  14 us
  transfers between devices with their start and end apart: 4, of which 4 were waited for; matrix products, arithmetic and copies ran while one was open for 0% of the time, Pallas kernels for 0%

commit v1 on v0

--- a/solution.py
+++ b/solution.py
@@ -1,9 +1,73 @@
 import jax
 import jax.numpy as jnp
 from jax import lax
+from jax.experimental import pallas as pl
+from jax.experimental.pallas import tpu as pltpu
 from jax.sharding import PartitionSpec as P
 
 PANEL = 512
+HI = lax.Precision.HIGHEST
+
+TILE=128
+SUB=8
+
+def factor_tile(a):
+    groups=TILE//SUB
+    rows=lax.broadcasted_iota(jnp.int32,(SUB,TILE),0)
+    lanes=lax.broadcasted_iota(jnp.int32,(SUB,TILE),1)
+    left=[a[g*SUB:(g+1)*SUB,:] for g in range(groups)]
+    right=[jnp.where(lanes==rows+g*SUB,1.0,0.0).astype(jnp.float32) for g in range(groups)]
+    spread=lambda x,j: jnp.broadcast_to(x[:,j:j+1],(SUB,TILE))
+    flat=lambda x,i: jnp.broadcast_to(x[i:i+1,:],(SUB,TILE))
+    col=[spread(x,0) for x in left]
+    pivots=[jnp.ones((SUB,TILE),jnp.float32) for _ in range(groups)]
+    for j in range(TILE):
+        g0,i0=divmod(j,SUB)
+        d=flat(col[g0],i0)
+        inv=1.0/d
+        pivots[g0]=jnp.where(rows==i0,d,pivots[g0])
+        if j==TILE-1: break
+        g1,i1=divmod(j+1,SUB)
+        nxt=[spread(left[g],j+1) if g>=g1 else None for g in range(groups)]
+        c1=flat(col[g1],i1)
+        lrow=flat(left[g0],i0); rrow=flat(right[g0],i0)
+        new=[None]*groups
+        for g in range(g0,groups):
+            m=col[g]*inv
+            if g==g0: m=jnp.where(rows>i0,m,0.0)
+            if g>=g1: new[g]=nxt[g]-m*c1
+            left[g]=left[g]-m*lrow
+            right[g]=right[g]-m*rrow
+        col=new
+    return jnp.concatenate([r*lax.rsqrt(p) for r,p in zip(right,pivots)],axis=0)
+
+def inverse_kernel(a_ref,x_ref,work):
+    n=a_ref.shape[0]; tiles=n//TILE
+    r=lax.broadcasted_iota(jnp.int32,(n,n),0); c=lax.broadcasted_iota(jnp.int32,(n,n),1)
+    work[...]=a_ref[...]
+    x_ref[...]=jnp.where(r==c,1.0,0.0).astype(jnp.float32)
+    def step(p,carry):
+        here=pl.ds(pl.multiple_of(p*TILE,TILE),TILE)
+        tile=factor_tile(work[here,here])
+        upper=jnp.dot(tile,work[here,:],precision=HI,preferred_element_type=jnp.float32)
+        solved=jnp.dot(tile,x_ref[here,:],precision=HI,preferred_element_type=jnp.float32)
+        x_ref[here,:]=solved
+        for q in range(1,tiles):
+            @pl.when(q>p)
+            def _():
+                below=slice(q*TILE,(q+1)*TILE)
+                w=upper[:,below]
+                ct=(((0,),(0,)),((),()))
+                work[below,:]-=lax.dot_general(w,upper,ct,precision=HI,preferred_element_type=jnp.float32)
+                x_ref[below,:]-=lax.dot_general(w,solved,ct,precision=HI,preferred_element_type=jnp.float32)
+        return carry
+    lax.fori_loop(0,tiles,step,0)
+
+def inverse_factor(a):
+    n=a.shape[0]
+    return pl.pallas_call(inverse_kernel,out_shape=jax.ShapeDtypeStruct((n,n),jnp.float32),
+        in_specs=[pl.BlockSpec(memory_space=pltpu.VMEM)],out_specs=pl.BlockSpec(memory_space=pltpu.VMEM),
+        scratch_shapes=[pltpu.VMEM((n,n),jnp.float32)],name="inverse_factor")(a)
 
 
 def broadcast(value, axis, source):
@@ -43,9 +107,9 @@
     pivot_source = gathered[:, :PANEL]
     block_source = lax.dynamic_slice_in_dim(gathered, cone_place * PANEL, PANEL, 1)
     pivot_matrix = (pivot_source + pivot_source.T) * 0.5
-    lower_factor = jnp.linalg.cholesky(pivot_matrix)
+    inverse = inverse_factor(pivot_matrix)
     combined = jnp.concatenate([panel_block, block_source], axis=1)
-    solved = jax.scipy.linalg.solve_triangular(lower_factor, combined, lower=True)
+    solved = jnp.dot(inverse, combined, precision=HI)
     factor_rows = solved[:, :per_block]
     row_factor = solved[:, per_block:]
     updated = schur_slab - jnp.einsum(

time: 497 us -> 362 us (0.73); the launches traced: 488 us -> 361 us
  other arithmetic: 132 us -> 9.63 us
  Pallas kernels: 0 us -> 30 us
  matrix products: 54.8 us -> 38.9 us
  local copies, waits for them, and re-layouts: 33.7 us -> 18.2 us
    another operation x18 -> x0, other arithmetic: 123 us -> none  [the longest x14 80.8 us: shards(): lower_factor = jnp.linalg.cholesky(pivot_matrix)]
    pallas_call x0 -> x1, Pallas kernels: none -> 30 us  [inverse_factor(): pl.pallas_call(inverse_kernel, out_shape=jax.ShapeDtypeStruct((n, n), jnp...]
    another operation x13 -> x0, matrix products: 26.7 us -> none  [the longest x7 18.8 us: shards(): jax.scipy.linalg.solve_triangular(lower_factor, combined, lower=True)]
    another operation x20 -> x0, local copies, waits for them, and re-layouts: 22 us -> none
    dot_general x0 -> x1, matrix products: none -> 7.29 us  [shards(): solved = jnp.dot(inverse, combined, precision=HI)]
where the time goes in v1:
time: 362 us; the launch traced here: 361 us
  waiting for transfers between devices  251 us (69%)
  matrix products  38.9 us (11%)
  Pallas kernels  30 us (8%)
  local copies, waits for them, and re-layouts  18.2 us (5%)
  between operations  13.2 us (4%)
  other arithmetic  9.63 us (3%)
    reduce_scatter x1, waiting for transfers between devices, shards(): lax.psum_scatter(gram_primal * gram_dual, 'cone', scatter_dimension=0, ti...  85.2 us
    psum x1, waiting for transfers between devices, broadcast(): return lax.psum(kept, axis)  69.2 us
    all_gather x1, waiting for transfers between devices, shards(): lax.all_gather(own_vectors[:row_dev], 'con', axis=0, tiled=True)  49.7 us
    all_gather x1, waiting for transfers between devices, shards(): gathered = lax.all_gather(leading_columns, 'con', axis=1, tiled=True)  47 us
    pallas_call x1, Pallas kernels, inverse_factor(): pl.pallas_call(inverse_kernel, out_shape=jax.ShapeDtypeStruct((n, n), jnp...  30 us
    dot_general x1, matrix products, shards(): jnp.einsum('kr,kc->rc', row_factor, factor_rows, precision=lax.Precision....  8.43 us
    unnamed x14, local copies, waits for them, and re-layouts  7.39 us
    dot_general x1, matrix products, shards(): solved = jnp.dot(inverse, combined, precision=HI)  7.29 us
  transfers between devices with their start and end apart: 4, of which 4 were waited for; matrix products, arithmetic and copies ran while one was open for 0% of the time, Pallas kernels for 0%

profile of v1, /device:TPU:0, one launch (start us, length us, event | category | flops | bytes accessed | tf_op | source)
XLA Modules:
  0.0 361.4 jit_solution(15309607640109397533)
XLA Ops:
  6.5 0.0 copy-start
  6.5 0.0 all-gather.6.cloned.1.call-start
  6.5 1.4 fusion.20
  7.9 2.4 broadcast_multiply_fusion
  10.3 0.0 copy-start.2
  10.3 1.3 copy-done.2
  11.6 0.8 slice.24
  12.4 0.0 all-gather.6.cloned.1.call-update
  12.5 0.0 reduce-scatter.2.cloned.1.call-start
  12.5 49.7 %all-gather.6.cloned.1.call-done = bf16[1,2048,1024]{2,1,0:T(8,128)(2,1)} async-done(((bf16[1,256,1024]{2,1,0:T(8,128)(2,1)}), bf16[1,2048,1024]{2,1,0:T(8,128)(2,1)}) %all-gather.6.cloned.1.call-update) | async-done | bytes 4194320 | tf_op jit(solution)/shard_map/all_gather | solution.py:91
  62.2 0.0 copy-done
  62.2 0.0 copy-start.3
  62.2 7.1 %fusion.2 = bf16[2048,1024]{1,0:T(8,128)(2,1)S(1)} fusion(bf16[1,2048,1024]{2,1,0:T(8,128)(2,1)} %all-gather.6.cloned.1.call-done, bf16[1,1024,1024]{2,1,0:T(8,128)(2,1)S(1)} %copy-done), kind=kOutput, calls=%fused_computation.3 | convolution fusion | flops 4294967296 | bytes 10485760 | tf_op jit(solution)/shard_map/dot_general | solution.py:92
  69.3 0.0 copy-done.3
  69.3 0.0 copy-start.4
  69.3 0.0 copy-start.5
  69.3 4.6 %fusion.5 = f32[2048,1024]{0,1:T(8,128)S(1)} fusion(bf16[2048,1024]{1,0:T(8,128)(2,1)S(1)} %fusion.2, bf16[1,1024,1024]{2,1,0:T(8,128)(2,1)S(1)} %copy-done.3), kind=kOutput, calls=%fused_computation.6 | convolution fusion | flops 4294967296 | bytes 14680064 | tf_op jit(solution)/shard_map/dot_general | solution.py:99
  73.9 0.0 copy-done.4
  73.9 0.0 copy-done.5
  73.9 4.8 %fusion = bf16[2048,1024]{1,0:T(8,128)(2,1)S(1)} fusion(bf16[1,2048,1024]{2,1,0:T(8,128)(2,1)S(1)} %copy-done.4, bf16[1,1024,1024]{2,1,0:T(8,128)(2,1)S(1)} %copy-done.5), kind=kOutput, calls=%fused_computation.1 | convolution fusion | flops 4294967296 | bytes 10485760 | tf_op jit(solution)/shard_map/dot_general | solution.py:95
  78.7 6.8 %convolution_multiply_fusion = f32[2048,1024]{0,1:T(8,128)} fusion(f32[2048,1024]{0,1:T(8,128)S(1)} %fusion.5, bf16[2048,1024]{1,0:T(8,128)(2,1)S(1)} %fusion, bf16[1,1024,1024]{2,1,0:T(8,128)(2,1)S(1)} %copy-done.3), kind=kOutput, calls=%fused_computation | convolution fusion | flops 4297064448 | bytes 23068672 | tf_op jit(solution)/shard_map/dot_general | solution.py:102
  85.5 0.0 reduce-scatter.2.cloned.1.call-update
  85.5 0.0 all-reduce.2.cloned.1.call-start
  85.6 85.2 %reduce-scatter.2.cloned.1.call-done = f32[512,1024]{0,1:T(8,128)} async-done(((f32[2048,1024]{0,1:T(8,128)}), f32[512,1024]{0,1:T(8,128)}) %reduce-scatter.2.cloned.1.call-update) | async-done | bytes 2097168 | tf_op jit(solution)/shard_map/reduce_scatter | solution.py:103
  170.7 3.1 broadcast_select_fusion
  173.9 0.0 all-reduce.2.cloned.1.call-update
  173.9 0.2 all-gather.4.cloned.1.call-start
  174.1 69.2 %all-reduce.2.cloned.1.call-done = f32[512,1024]{0,1:T(8,128)} async-done(((f32[512,1024]{0,1:T(8,128)}), f32[512,1024]{0,1:T(8,128)}) %all-reduce.2.cloned.1.call-update) | async-done | bytes 2097168 | tf_op jit(solution)/shard_map/psum | solution.py:75
  243.4 1.9 slice.25
  245.2 0.0 all-gather.4.cloned.1.call-update
  245.3 47.0 %all-gather.4.cloned.1.call-done = f32[512,2048]{0,1:T(8,128)} async-done(((f32[512,256]{0,1:T(8,128)}), f32[512,2048]{0,1:T(8,128)}) %all-gather.4.cloned.1.call-update) | async-done | bytes 4194320 | tf_op jit(solution)/shard_map/all_gather | solution.py:106
  292.3 2.7 constant_dynamic-slice_fusion
  295.0 2.6 copy.7
  297.5 2.7 fusion.16.a_ref
  300.3 30.0 %inverse_factor.1 = f32[512,512]{1,0:T(8,128)} custom-call(f32[512,512]{1,0:T(8,128)} %fusion.16.a_ref), custom_call_target="tpu_custom_call" | custom-call | tf_op jit(solution)/shard_map/inverse_factor/pallas_call | solution.py:68
  330.2 7.3 %fusion.7 = f32[512,1536]{1,0:T(8,128)S(1)} fusion(f32[512,512]{1,0:T(8,128)} %inverse_factor.1, f32[512,512]{0,1:T(8,128)S(1)} %get-tuple-element.5, f32[512,1024]{0,1:T(8,128)} %all-reduce.2.cloned.1.call-done), kind=kOutput, calls=%fused_computation.8 | convolution fusion | flops 4832624640 | bytes 7340032 | tf_op jit(solution)/shard_map/dot_general | solution.py:112
  337.5 0.0 copy-start.1
  337.5 1.6 copy-done.1
  339.2 1.5 slice.27
  340.7 2.9 copy.14
  343.6 8.4 %select_select_fusion = f32[512,1024]{0,1:T(8,128)} fusion(f32[512,1024]{0,1:T(8,128)} %copy.14, f32[512,1024]{0,1:T(8,128)} %reduce-scatter.2.cloned.1.call-done, f32[512,1536]{1,0:T(8,128)} %copy-done.1, pred[1024]{0:T(1024)(128)(4,1)S(1)} %fusion.17, pred[]{:T(512)S(6)} %eq.4), kind=kOutput, calls=%fused_computation.16 | convolution fusion | flops 3222798336 | bytes 9438209 | tf_op jit(solution)/shard_map/kr,kc->rc/dot_general | solution.py:115
  352.0 2.9 copy.10
  (1 shorter events, 0.0 us)
Async XLA Ops:
  6.5 55.7 %copy-start = (bf16[1,1024,1024]{2,1,0:T(8,128)(2,1)S(1)}, bf16[1,1024,1024]{2,1,0:T(8,128)(2,1)}, u32[]{:S(2)}) copy-start(bf16[1,1024,1024]{2,1,0:T(8,128)(2,1)} %param.5) | copy-start | bytes 6291460
  6.5 55.7 %all-gather.6.cloned.1.call-start = ((), (), s32[]{:S(2)}) async-start(), calls=%async_computation.4 | async-start | bytes 4718592 | tf_op jit(solution)/shard_map/all_gather | solution.py:91
  10.3 1.3 copy-start.2
  12.5 158.3 %reduce-scatter.2.cloned.1.call-start = ((), (), s32[]{:S(2)}) async-start(), calls=%async_computation.1 | async-start | bytes 10485760 | tf_op jit(solution)/shard_map/reduce_scatter | solution.py:103
  62.2 7.1 %copy-start.3 = (bf16[1,1024,1024]{2,1,0:T(8,128)(2,1)S(1)}, bf16[1,1024,1024]{2,1,0:T(8,128)(2,1)}, u32[]{:S(2)}) copy-start(bf16[1,1024,1024]{2,1,0:T(8,128)(2,1)} %copy-done.2) | copy-start | bytes 6291460
  69.3 4.6 %copy-start.4 = (bf16[1,2048,1024]{2,1,0:T(8,128)(2,1)S(1)}, bf16[1,2048,1024]{2,1,0:T(8,128)(2,1)}, u32[]{:S(2)}) copy-start(bf16[1,2048,1024]{2,1,0:T(8,128)(2,1)} %all-gather.6.cloned.1.call-done) | copy-start | bytes 12582916
  69.3 4.6 %copy-start.5 = (bf16[1,1024,1024]{2,1,0:T(8,128)(2,1)S(1)}, bf16[1,1024,1024]{2,1,0:T(8,128)(2,1)}, u32[]{:S(2)}) copy-start(bf16[1,1024,1024]{2,1,0:T(8,128)(2,1)} %param.6) | copy-start | bytes 6291460
  85.5 157.9 %all-reduce.2.cloned.1.call-start = ((), (), s32[]{:S(2)}) async-start(), calls=%async_computation.2 | async-start | bytes 4194304 | tf_op jit(solution)/shard_map/psum | solution.py:75
  173.9 118.4 %all-gather.4.cloned.1.call-start = ((), (), s32[]{:S(2)}) async-start(), calls=%async_computation.3 | async-start | bytes 4718592 | tf_op jit(solution)/shard_map/all_gather | solution.py:106
  337.5 1.6 copy-start.1
Sparse Core Ops, SparseCore 0:
  12.6 49.5 all-gather.5
  85.6 85.0 reduce-scatter.1
  174.0 69.3 all-reduce.1
  245.4 46.8 all-gather.3

commit v2 on v0

v2 whole, which is shorter than its diff:
```python
import functools
import math

import jax
import jax.numpy as jnp
from jax import lax
from jax.experimental import pallas as pl
from jax.experimental.pallas import tpu as pltpu
from jax.sharding import PartitionSpec as P

PANEL = 512
TILE = 128
SUB = 8
STEPS = 128
LEVELS = 32767.0
OCTAVE = math.log(2.0) / STEPS
HI = lax.Precision.HIGHEST
ROWS_T = (((1,), (1,)), ((), ()))
COLS_T = (((0,), (0,)), ((), ()))
F32 = jnp.float32
BF16 = jnp.bfloat16
I16 = jnp.int16


def in_vmem(count):
    return [pl.BlockSpec(memory_space=pltpu.VMEM)] * count


def in_smem():
    return pl.BlockSpec(memory_space=pltpu.SMEM)


def shaped(rows, columns, dtype):
    return jax.ShapeDtypeStruct((rows, columns), dtype)


def encode(value, out_ref, start):
    rows = value.shape[0]
    top = jnp.max(jnp.abs(value), axis=0, keepdims=True)
    level = jnp.ceil(jnp.log(jnp.maximum(top, 1e-37)) * (1.0 / OCTAVE))
    scaled = value * jnp.exp(level * -OCTAVE) * LEVELS
    whole = jnp.round(jnp.clip(scaled, -LEVELS, LEVELS)).astype(jnp.int32)
    out_ref[start : start + rows, :] = whole.astype(I16)
    levels = jnp.broadcast_to(level, (SUB, value.shape[1])).astype(jnp.int32)
    out_ref[start + rows : start + rows + SUB, :] = levels.astype(I16)


def decode(ref, start, rows):
    whole = ref[start : start + rows, :].astype(jnp.int32).astype(F32)
    level = ref[start + rows : start + rows + SUB, :].astype(jnp.int32).astype(F32)[0:1]
    return whole * (jnp.exp(level * OCTAVE) * (1.0 / LEVELS))


def factor_tile(a):
    groups = TILE // SUB
    rows = lax.broadcasted_iota(jnp.int32, (SUB, TILE), 0)
    lanes = lax.broadcasted_iota(jnp.int32, (SUB, TILE), 1)
    left = [a[g * SUB : (g + 1) * SUB, :] for g in range(groups)]
    right = [jnp.where(lanes == rows + g * SUB, 1.0, 0.0).astype(F32) for g in range(groups)]
    spread = lambda x, j: jnp.broadcast_to(x[:, j : j + 1], (SUB, TILE))
    flat = lambda x, i: jnp.broadcast_to(x[i : i + 1, :], (SUB, TILE))
    column = [spread(x, 0) for x in left]
    pivots = [jnp.ones((SUB, TILE), F32) for _ in range(groups)]
    for j in range(TILE):
        g0, i0 = divmod(j, SUB)
        pivot = flat(column[g0], i0)
        pivots[g0] = jnp.where(rows == i0, pivot, pivots[g0])
        if j == TILE - 1:
            break
        inverse = 1.0 / pivot
        g1, i1 = divmod(j + 1, SUB)
        ahead = [spread(left[g], j + 1) if g >= g1 else None for g in range(groups)]
        corner = flat(column[g1], i1)
        left_row = flat(left[g0], i0)
        right_row = flat(right[g0], i0)
        following = [None] * groups
        for g in range(g0, groups):
            ratio = column[g] * inverse
            if g == g0:
                ratio = jnp.where(rows > i0, ratio, 0.0)
            if g >= g1:
                following[g] = ahead[g] - ratio * corner
            left[g] = left[g] - ratio * left_row
            right[g] = right[g] - ratio * right_row
        column = following
    return jnp.concatenate([r * lax.rsqrt(p) for r, p in zip(right, pivots)], axis=0)


def inverse_kernel(place_ref, *refs):
    *half_refs, x_ref, work, square = refs
    size = x_ref.shape[0]
    tiles = size // TILE
    owners = len(half_refs)
    width = size // owners
    core = place_ref[2]
    for s, half_ref in enumerate(half_refs):
        where = lax.rem(core + s, owners) * width
        square[:, pl.ds(pl.multiple_of(where, TILE), width)] = half_ref[...]
    rows = lax.broadcasted_iota(jnp.int32, (size, size), 0)
    columns = lax.broadcasted_iota(jnp.int32, (size, size), 1)
    value = square[...]
    work[...] = (value + value.T) * 0.5
    x_ref[...] = jnp.where(rows == columns, 1.0, 0.0).astype(F32)

    def step(p, carry):
        here = pl.ds(pl.multiple_of(p * TILE, TILE), TILE)
        tile = factor_tile(work[here, here])
        upper = jnp.dot(tile, work[here, :], precision=HI, preferred_element_type=F32)
        solved = jnp.dot(tile, x_ref[here, :], precision=HI, preferred_element_type=F32)
        x_ref[here, :] = solved
        for q in range(1, tiles):

            @pl.when(q > p)
            def _():
                below = slice(q * TILE, (q + 1) * TILE)
                part = upper[:, below]
                work[below, :] -= lax.dot_general(
                    part, upper, COLS_T, precision=HI, preferred_element_type=F32
                )
                x_ref[below, :] -= lax.dot_general(
                    part, solved, COLS_T, precision=HI, preferred_element_type=F32
                )

        return carry

    lax.fori_loop(0, tiles, step, 0)


def inverse_factor(place, halves):
    size = halves[0].shape[0]
    return pl.pallas_call(
        inverse_kernel,
        out_shape=shaped(size, size, F32),
        in_specs=[in_smem()] + in_vmem(len(halves)),
        out_specs=pl.BlockSpec(memory_space=pltpu.VMEM),
        scratch_shapes=[pltpu.VMEM((size, size), F32)] * 2,
        name="inverse_factor",
    )(place, *halves)


def weigh(rows_ref, primal_ref, dual_ref):
    rows = rows_ref[...]
    by_primal = jnp.dot(rows, primal_ref[...], preferred_element_type=F32).astype(BF16)
    by_dual = jnp.dot(rows, dual_ref[...], preferred_element_type=F32).astype(BF16)
    return by_primal, by_dual


def hadamard(by_primal, by_dual, columns):
    return lax.dot_general(
        by_primal, columns, ROWS_T, preferred_element_type=F32
    ) * lax.dot_general(by_dual, columns, ROWS_T, preferred_element_type=F32)


def pivot_kernel(place_ref, rows_ref, primal_ref, dual_ref, own_ref, code_ref, p_ref, d_ref):
    by_primal, by_dual = weigh(rows_ref, primal_ref, dual_ref)
    p_ref[...] = by_primal
    d_ref[...] = by_dual
    width = own_ref.shape[1]
    mine = pl.ds(pl.multiple_of(place_ref[2] * width, width), width)
    value = hadamard(by_primal, by_dual, rows_ref[mine, :])
    own_ref[...] = value
    for g in range(value.shape[0] // TILE):
        encode(value[g * TILE : (g + 1) * TILE], code_ref, g * (TILE + SUB))


def scatter_terms(value_ref, place_ref, own_ref, code_refs):
    share = own_ref.shape[0]
    cone = place_ref[0]
    own_ref[...] = value_ref[pl.ds(pl.multiple_of(cone * share, share), share), :]
    for u, code_ref in enumerate(code_refs, 1):
        other = jnp.bitwise_xor(cone, u) * share
        encode(value_ref[pl.ds(pl.multiple_of(other, share), share), :], code_ref, 0)


def panel_terms_kernel(place_ref, p_ref, d_ref, columns_ref, own_ref, *rest):
    *code_refs, value_ref = rest
    flag = place_ref[3].astype(F32)
    value_ref[...] = hadamard(p_ref[...], d_ref[...], columns_ref[...]) * flag
    scatter_terms(value_ref, place_ref, own_ref, code_refs)


def terms_kernel(place_ref, rows_ref, primal_ref, dual_ref, columns_ref, own_ref, *rest):
    *code_refs, value_ref = rest
    flag = place_ref[3].astype(F32)
    by_primal, by_dual = weigh(rows_ref, primal_ref, dual_ref)
    value_ref[...] = hadamard(by_primal, by_dual, columns_ref[...]) * flag
    scatter_terms(value_ref, place_ref, own_ref, code_refs)


def sum_half_kernel(own_ref, *refs):
    *code_refs, out_ref = refs
    for g in range(own_ref.shape[0] // TILE):
        rows = slice(g * TILE, (g + 1) * TILE)
        total = own_ref[rows, :]
        for code_ref in code_refs:
            total = total + decode(code_ref, g * (TILE + SUB), TILE)
        out_ref[rows, :] = total


def sum_panel_kernel(own_ref, *refs):
    *code_refs, sum_ref, out_ref = refs
    total = own_ref[...]
    for code_ref in code_refs:
        total = total + decode(code_ref, 0, total.shape[0])
    sum_ref[...] = total
    encode(total, out_ref, 0)


def sum_rest_kernel(cones, place_ref, *refs):
    blocks = cones - 1
    cone = place_ref[0]
    inputs = refs[: blocks * cones]
    own_ref, *code_refs = refs[blocks * cones : blocks * cones + cones]
    sums = refs[-1]
    for b in range(blocks):
        first, *codes = inputs[b * cones : (b + 1) * cones]
        total = first[...]
        for code in codes:
            total = total + decode(code, 0, total.shape[0])
        sums[b + 1] = total
    sums[0] = jnp.zeros_like(sums[0])
    own_ref[...] = sums[cone]
    for u, code_ref in enumerate(code_refs, 1):
        encode(sums[jnp.bitwise_xor(cone, u)], code_ref, 0)


def gather_panel_kernel(place_ref, own_ref, *refs):
    *code_refs, panel_ref, lead_ref = refs
    share = own_ref.shape[0]
    cone = place_ref[0]
    panel_ref[pl.ds(pl.multiple_of(cone * share, share), share), :] = own_ref[...]
    for u, code_ref in enumerate(code_refs, 1):
        other = jnp.bitwise_xor(cone, u) * share
        panel_ref[pl.ds(pl.multiple_of(other, share), share), :] = decode(code_ref, 0, share)
    width = lead_ref.shape[1]
    for g in range(panel_ref.shape[0] // TILE):
        encode(panel_ref[g * TILE : (g + 1) * TILE, :width], lead_ref, g * (TILE + SUB))


def rows_kernel(place_ref, inverse_ref, panel_ref, *refs):
    *lead_refs, factor_ref, row_ref, lead = refs
    owners = len(lead_refs)
    width = lead_refs[0].shape[1]
    core = place_ref[2]
    for s, lead_ref in enumerate(lead_refs):
        where = pl.ds(pl.multiple_of(lax.rem(core + s, owners) * width, width), width)
        for g in range(panel_ref.shape[0] // TILE):
            lead[g * TILE : (g + 1) * TILE, where] = decode(lead_ref, g * (TILE + SUB), TILE)
    inverse = inverse_ref[...]
    factor_ref[...] = jnp.dot(inverse, panel_ref[...], precision=HI, preferred_element_type=F32)
    row_ref[...] = jnp.dot(inverse, lead[...], precision=HI, preferred_element_type=F32)


def update_kernel(place_ref, factor_ref, row_ref, own_ref, *refs):
    *code_refs, out_ref = refs
    share = own_ref.shape[0]
    cone = place_ref[0]

    @pl.when(cone == 0)
    def _():
        out_ref[...] = factor_ref[...]

    @pl.when(cone != 0)
    def _():
        out_ref[pl.ds(pl.multiple_of(cone * share, share), share), :] = own_ref[...]
        for u, code_ref in enumerate(code_refs, 1):
            other = jnp.bitwise_xor(cone, u) * share
            out_ref[pl.ds(pl.multiple_of(other, share), share), :] = decode(code_ref, 0, share)
        change = lax.dot_general(
            row_ref[...], factor_ref[...], COLS_T, precision=HI, preferred_element_type=F32
        )
        columns = lax.broadcasted_iota(jnp.int32, out_ref.shape, 1)
        dropped = (columns < place_ref[5]) & (place_ref[4] != 0)
        out_ref[...] = jnp.where(dropped, 0.0, out_ref[...] - change)


def call(kernel, out_shape, place, operands, scratch=(), name=None):
    specs = in_vmem(len(operands))
    if place is not None:
        specs = [in_smem()] + specs
        operands = (place, *operands)
    return pl.pallas_call(
        kernel,
        out_shape=out_shape,
        in_specs=specs,
        out_specs=jax.tree.map(lambda _: pl.BlockSpec(memory_space=pltpu.VMEM), out_shape),
        scratch_shapes=scratch,
        name=name,
    )(*operands)


def shards(vectors, primal, dual_inverse, touches):
    con_count = lax.axis_size("con")
    cones = lax.axis_size("cone")
    con_place = lax.axis_index("con")
    cone_place = lax.axis_index("cone")
    per_block = vectors.shape[1]
    row_dev = PANEL * cones // con_count
    owners = con_count // cones
    share = PANEL // cones
    chip, core = con_place // owners, con_place % owners
    flag = lax.dynamic_index_in_dim(touches[0], con_place, 0, keepdims=False)
    place = jnp.stack(
        [
            cone_place,
            con_place,
            core,
            flag,
            (con_place < owners).astype(jnp.int32),
            jnp.int32(row_dev),
        ]
    ).astype(jnp.int32)
    columns, primal_block, dual_block = vectors[0], primal[0], dual_inverse[0]

    def across(value, u):
        return lax.ppermute(value, "cone", [(i, i ^ u) for i in range(cones)])

    def beside(value, s):
        pairs = [
            (g * owners + i, g * owners + (i - s) % owners)
            for g in range(cones)
            for i in range(owners)
        ]
        return lax.ppermute(value, "con", pairs)

    def exchange(codes):
        return [across(code, u) for u, code in enumerate(codes, 1)]

    own_rows = columns[:row_dev] * flag.astype(BF16)
    gathered = lax.all_gather(own_rows, "con", axis=0, tiled=True)
    blocks = [gathered[b * PANEL : (b + 1) * PANEL] for b in range(cones)]

    coded_square = (PANEL // TILE) * (TILE + SUB)
    half_own, half_code, by_primal, by_dual = call(
        pivot_kernel,
        (
            shaped(PANEL, row_dev, F32),
            shaped(coded_square, row_dev, I16),
            shaped(*blocks[0].shape, BF16),
            shaped(*blocks[0].shape, BF16),
        ),
        place,
        (blocks[0], primal_block, dual_block),
        name="pivot",
    )
    half_codes = [across(half_code, u) for u in range(1, cones)]

    terms_shape = (shaped(share, per_block, F32),) + (shaped(share + SUB, per_block, I16),) * (
        cones - 1
    )
    scratch = [pltpu.VMEM((PANEL, per_block), F32)]
    first, *codes = call(
        panel_terms_kernel, terms_shape, place, (by_primal, by_dual, columns), scratch, "panel_terms"
    )
    panel_parts = [first] + exchange(codes)
    rest_parts = []
    for b in range(1, cones):
        first, *codes = call(
            terms_kernel,
            terms_shape,
            place,
            (blocks[b], primal_block, dual_block, columns),
            scratch,
            f"terms_{b}",
        )
        rest_parts += [first] + exchange(codes)

    half = call(
        sum_half_kernel, shaped(PANEL, row_dev, F32), None, (half_own, *half_codes), name="sum_half"
    )
    halves = [half] + [beside(half, s) for s in range(1, owners)]
    inverse = inverse_factor(place, halves)

    panel_own, panel_code = call(
        sum_panel_kernel,
        (shaped(share, per_block, F32), shaped(share + SUB, per_block, I16)),
        None,
        panel_parts,
        name="sum_panel",
    )
    panel_codes = [across(panel_code, u) for u in range(1, cones)]
    panel, lead = call(
        gather_panel_kernel,
        (shaped(PANEL, per_block, F32), shaped(coded_square, row_dev, I16)),
        place,
        (panel_own, *panel_codes),
        name="gather_panel",
    )
    mine = jnp.where(chip == cone_place, lead, jnp.zeros_like(lead))
    for d in range(1, cones):
        pairs = [
            (c * con_count + c * owners + i, c * con_count + (c ^ d) * owners + i)
            for c in range(1, cones)
            for i in range(owners)
        ]
        mine = mine + lax.ppermute(lead, ("cone", "con"), pairs)
    leads = [mine] + [beside(mine, s) for s in range(1, owners)]


    rest_own, *rest_codes = call(
        functools.partial(sum_rest_kernel, cones),
        terms_shape,
        place,
        rest_parts,
        [pltpu.VMEM((cones, share, per_block), F32)],
        "sum_rest",
    )
    rest_codes = [
        lax.ppermute(code, "cone", [(i, i ^ u) for i in range(cones) if i ^ u])
        for u, code in enumerate(rest_codes, 1)
    ]
    factor_rows, row_factor = call(
        rows_kernel,
        (shaped(PANEL, per_block, F32), shaped(PANEL, PANEL, F32)),
        place,
        (inverse, panel, *leads),
        [pltpu.VMEM((PANEL, PANEL), F32)],
        "rows",
    )
    return call(
        update_kernel,
        shaped(PANEL, per_block, F32),
        place,
        (factor_rows, row_factor, rest_own, *rest_codes),
        name="update",
    )


def solution(mesh):
    in_specs = (
        P("cone", "con", None),
        P("cone", None, None),
        P("cone", None, None),
        P("cone", None),
    )
    out_specs = P("cone", "con")
    return jax.shard_map(shards, mesh=mesh, in_specs=in_specs, out_specs=out_specs, check_vma=False)
```

time: 497 us -> 225 us (0.45)
  the two profiles are of different devices: /device:TPU:0 before, /device:TPU:21 now
where the time goes in v2:
time: 225 us
  Pallas kernels  98.4 us (44%)
  waiting for transfers between devices  58.7 us (26%)
  starting transfers between devices  39.9 us (18%)
  between operations  13.7 us (6%)
  local copies, waits for them, and re-layouts  9.06 us (4%)
  other arithmetic  4.87 us (2%)
    pallas_call x11, Pallas kernels, call(): pl.pallas_call(kernel, out_shape=out_shape, in_specs=specs, out_specs=jax...  68.1 us
    all_gather x1, waiting for transfers between devices, shards(): gathered = lax.all_gather(own_rows, 'con', axis=0, tiled=True)  46 us
    pallas_call x1, Pallas kernels, inverse_factor(): pl.pallas_call(inverse_kernel, out_shape=shaped(size, size, F32), in_spec...  30.3 us
    ppermute x18, starting transfers between devices, across(): return lax.ppermute(value, 'cone', [(i, i ^ u) for i in range(cones)])  16.7 us
    ppermute x18, waiting for transfers between devices, across(): return lax.ppermute(value, 'cone', [(i, i ^ u) for i in range(cones)])  12.7 us
    ppermute x3, starting transfers between devices, shards(): lax.ppermute(code, 'cone', [(i, i ^ u) for i in range(cones) if i ^ u])  11.4 us
    ppermute x3, starting transfers between devices, shards(): mine = mine + lax.ppermute(lead, ('cone', 'con'), pairs)  6.85 us
    ppermute x2, starting transfers between devices, beside(): return lax.ppermute(value, 'con', pairs)  4.99 us
  transfers between devices with their start and end apart: 27, of which 5 were waited for; matrix products, arithmetic and copies ran while one was open for 1% of the time, Pallas kernels for 35%

profile of v2, /device:TPU:21, one launch (start us, length us, event | category | flops | bytes accessed | tf_op | source)
XLA Modules:
  0.0 224.6 jit_solution(18162236014372081988)
XLA Ops:
  6.5 1.3 fusion
  7.9 2.4 %slice_multiply_fusion = bf16[1,256,1024]{2,1,0:T(8,128)(2,1)} fusion(bf16[1,1024,1024]{2,1,0:T(8,128)(2,1)} %param.4, bf16[]{:T(256)} %bitcast.5), kind=kLoop, calls=%fused_computation.4 | loop fusion | flops 262144 | bytes 1048578 | tf_op jit(solution)/shard_map/mul | solution.py:329
  10.3 0.0 all-gather.3.cloned.1.call-update
  10.3 1.3 stack.24.place_ref
  11.6 46.0 %all-gather.3.cloned.1.call-done = bf16[1,2048,1024]{2,1,0:T(8,128)(2,1)} async-done(((bf16[1,256,1024]{2,1,0:T(8,128)(2,1)}), bf16[1,2048,1024]{2,1,0:T(8,128)(2,1)}) %all-gather.3.cloned.1.call-update) | async-done | bytes 4194320 | tf_op jit(solution)/shard_map/all_gather | solution.py:330
  57.6 4.3 %slice_bitcast_fusion = (bf16[512,1024]{1,0:T(8,128)(2,1)}, bf16[512,1024]{1,0:T(8,128)(2,1)}, bf16[512,1024]{1,0:T(8,128)(2,1)}, bf16[512,1024]{1,0:T(8,128)(2,1)}) fusion(bf16[1,2048,1024]{2,1,0:T(8,128)(2,1)} %all-gather.3.cloned.1.call-done), kind=kLoop, calls=%fused_computation | loop fusion | bytes 8388608 | tf_op jit(solution)/shard_map/slice | solution.py:331
  61.8 6.7 %pivot.1 = (f32[512,256]{1,0:T(8,128)}, s16[544,256]{1,0:T(8,128)(2,1)}, bf16[512,1024]{1,0:T(8,128)(2,1)}, bf16[512,1024]{1,0:T(8,128)(2,1)}) custom-call(s32[6]{0:T(128)} %stack.24.place_ref, bf16[512,1024]{1,0:T(8,128)(2,1)} %get-tuple-element.68.rows_ref, bf16[1024,1024]{1,0:T(8,128)(2,1)} %bitcast.21, bf16[1024,1024]{1,0:T(8,128)(2,1)} %bitcast.25), custom_call_target="tpu_custom_call" | custom-call | tf_op jit(solution)/shard_map/pivot/pallas_call | solution.py:282
  68.5 5.9 %panel_terms.1 = (f32[128,1024]{1,0:T(8,128)}, s16[136,1024]{1,0:T(8,128)(2,1)}, s16[136,1024]{1,0:T(8,128)(2,1)}, s16[136,1024]{1,0:T(8,128)(2,1)}) custom-call(s32[6]{0:T(128)} %stack.24.place_ref, bf16[512,1024]{1,0:T(8,128)(2,1)} %get-tuple-element.37.p_ref, bf16[512,1024]{1,0:T(8,128)(2,1)} %get-tuple-element.38.d_ref, bf16[1024,1024]{1,0:T(8,128)(2,1)} %bitcast.17), custom_call_target="tpu_custom_call" | custom-call | tf_op jit(solution)/shard_map/panel_terms/pallas_call | solution.py:282
  74.5 1.2 collective-permute-start.4
  75.7 0.3 collective-permute-start.5
  75.9 1.2 collective-permute-start.6
  77.1 9.0 %terms_3.1 = (f32[128,1024]{1,0:T(8,128)}, s16[136,1024]{1,0:T(8,128)(2,1)}, s16[136,1024]{1,0:T(8,128)(2,1)}, s16[136,1024]{1,0:T(8,128)(2,1)}) custom-call(s32[6]{0:T(128)} %stack.24.place_ref, bf16[512,1024]{1,0:T(8,128)(2,1)} %get-tuple-element.65.rows_ref, bf16[1024,1024]{1,0:T(8,128)(2,1)} %bitcast.22, bf16[1024,1024]{1,0:T(8,128)(2,1)} %bitcast.26, ...), custom_call_target="tpu_custom_call" | custom-call | tf_op jit(solution)/shard_map/terms_3/pallas_call | solution.py:282
  86.2 1.2 collective-permute-start.20
  87.4 0.3 collective-permute-start.21
  87.6 0.0 collective-permute-done.4.refs_0_
  87.6 1.2 collective-permute-start.22
  88.8 9.0 %terms_2.1 = (f32[128,1024]{1,0:T(8,128)}, s16[136,1024]{1,0:T(8,128)(2,1)}, s16[136,1024]{1,0:T(8,128)(2,1)}, s16[136,1024]{1,0:T(8,128)(2,1)}) custom-call(s32[6]{0:T(128)} %stack.24.place_ref, bf16[512,1024]{1,0:T(8,128)(2,1)} %get-tuple-element.66.rows_ref, bf16[1024,1024]{1,0:T(8,128)(2,1)} %bitcast.23, bf16[1024,1024]{1,0:T(8,128)(2,1)} %bitcast.27, ...), custom_call_target="tpu_custom_call" | custom-call | tf_op jit(solution)/shard_map/terms_2/pallas_call | solution.py:282
  97.8 0.0 collective-permute-done.5.refs_1_
  97.8 1.3 collective-permute-start.17
  99.1 0.0 collective-permute-done.6.refs_2_
  99.1 0.3 collective-permute-start.18
  99.4 0.4 copy-done.20
  99.8 2.7 %sum_panel.1 = (f32[128,1024]{1,0:T(8,128)}, s16[136,1024]{1,0:T(8,128)(2,1)}) custom-call(f32[128,1024]{1,0:T(8,128)} %get-tuple-element.39.own_ref, s16[136,1024]{1,0:T(8,128)(2,1)} %copy-done.18, s16[136,1024]{1,0:T(8,128)(2,1)} %copy-done.19, s16[136,1024]{1,0:T(8,128)(2,1)} %copy-done.20), custom_call_target="tpu_custom_call" | custom-call | tf_op jit(solution)/shard_map/sum_panel/pallas_call | solution.py:282
  102.5 0.0 collective-permute-done.20.refs_9_
  102.5 0.8 collective-permute-start.9
  103.3 0.7 collective-permute-start.8
  104.0 0.0 collective-permute-done.22.refs_11_
  104.0 1.2 collective-permute-start.7
  105.2 9.0 %terms_1.1 = (f32[128,1024]{1,0:T(8,128)}, s16[136,1024]{1,0:T(8,128)(2,1)}, s16[136,1024]{1,0:T(8,128)(2,1)}, s16[136,1024]{1,0:T(8,128)(2,1)}) custom-call(s32[6]{0:T(128)} %stack.24.place_ref, bf16[512,1024]{1,0:T(8,128)(2,1)} %get-tuple-element.67.rows_ref, bf16[1024,1024]{1,0:T(8,128)(2,1)} %bitcast.24, bf16[1024,1024]{1,0:T(8,128)(2,1)} %bitcast.28, ...), custom_call_target="tpu_custom_call" | custom-call | tf_op jit(solution)/shard_map/terms_1/pallas_call | solution.py:282
  114.3 0.0 collective-permute-done.17.refs_5_
  114.3 0.8 collective-permute-start.19
  115.1 0.0 collective-permute-done.18.refs_6_
  115.1 1.2 collective-permute-start.14
  116.3 0.0 collective-permute-done.9.refs_2_
  116.3 0.7 collective-permute-start.2
  117.0 1.3 collective-permute-done.8.refs_1_
  118.4 0.5 collective-permute-start.1
  118.9 1.4 collective-permute-start
  120.2 3.0 %gather_panel.1 = (f32[512,1024]{1,0:T(8,128)}, s16[544,256]{1,0:T(8,128)(2,1)}) custom-call(s32[6]{0:T(128)} %stack.24.place_ref, f32[128,1024]{1,0:T(8,128)} %get-tuple-element.43.own_ref, s16[136,1024]{1,0:T(8,128)(2,1)} %copy-done.17, s16[136,1024]{1,0:T(8,128)(2,1)} %copy-done.16, s16[136,1024]{1,0:T(8,128)(2,1)} %copy-done.15), custom_call_target="tpu_custom_call" | custom-call | tf_op jit(solution)/shard_map/gather_panel/pallas_call | solution.py:282
  123.2 1.2 collective-permute-start.15
  124.4 4.8 %collective-permute-done.14.refs_1_ = s16[136,1024]{1,0:T(8,128)(2,1)S(1)} collective-permute-done((s16[136,1024]{1,0:T(8,128)(2,1)}, s16[136,1024]{1,0:T(8,128)(2,1)S(1)}, u32[]{:S(2)}, u32[]{:S(2)}) %collective-permute-start.14) | collective-permute-done | bytes 278560 | tf_op jit(solution)/shard_map/ppermute | solution.py:316
  129.2 1.4 collective-permute-start.16
  130.6 4.5 %collective-permute-done.2.refs_2_ = s16[544,256]{1,0:T(8,128)(2,1)S(1)} collective-permute-done((s16[544,256]{1,0:T(8,128)(2,1)}, s16[544,256]{1,0:T(8,128)(2,1)S(1)}, u32[]{:S(2)}, u32[]{:S(2)}) %collective-permute-start.2) | collective-permute-done | bytes 278560 | tf_op jit(solution)/shard_map/ppermute | solution.py:316
  135.1 2.1 collective-permute-start.12
  137.2 1.9 collective-permute-start.11
  139.1 2.1 collective-permute-done.refs_0_
  141.2 2.8 %collective-permute-start.10 = (s16[544,256]{1,0:T(8,128)(2,1)}, s16[544,256]{1,0:T(8,128)(2,1)}, u32[]{:S(2)}, u32[]{:S(2)}) collective-permute-start(s16[544,256]{1,0:T(8,128)(2,1)} %get-tuple-element.46), channel_id=1, source_target_pairs={{10,8},{11,9},{20,22},{21,23},{30,28},{31,29}} | collective-permute-start | bytes 835592 | tf_op jit(solution)/shard_map/ppermute | solution.py:396
  144.1 2.3 %sum_half.1.refs_0_ = f32[512,256]{1,0:T(8,128)} custom-call(f32[512,256]{1,0:T(8,128)} %get-tuple-element.35.own_ref, s16[544,256]{1,0:T(8,128)(2,1)} %copy-done.14, s16[544,256]{1,0:T(8,128)(2,1)} %copy-done.13, s16[544,256]{1,0:T(8,128)(2,1)} %copy-done.11), custom_call_target="tpu_custom_call" | custom-call | tf_op jit(solution)/shard_map/sum_half/pallas_call | solution.py:282
  146.4 4.9 %collective-permute-start.3 = (f32[512,256]{1,0:T(8,128)}, f32[512,256]{1,0:T(8,128)S(1)}, u32[]{:S(2)}, u32[]{:S(2)}) collective-permute-start(f32[512,256]{1,0:T(8,128)} %sum_half.1.refs_0_), channel_id=1, source_target_pairs={{0,1},{1,0},{2,3},{3,2},{4,5},{5,4},{6,7},{7,6},{8,9},{9,8},{10,11... | collective-permute-start | bytes 1572872 | tf_op jit(solution)/shard_map/ppermute | solution.py:324
  151.3 0.7 copy-done.12
  152.0 4.6 %sum_rest.1 = (f32[128,1024]{1,0:T(8,128)}, s16[136,1024]{1,0:T(8,128)(2,1)}, s16[136,1024]{1,0:T(8,128)(2,1)}, s16[136,1024]{1,0:T(8,128)(2,1)}) custom-call(s32[6]{0:T(128)} %stack.24.place_ref, f32[128,1024]{1,0:T(8,128)} %get-tuple-element.49.refs_0_, s16[136,1024]{1,0:T(8,128)(2,1)} %copy-done.8, s16[136,1024]{1,0:T(8,128)(2,1)} %copy-done.10, ...), custom_call_target="tpu_custom_call" | custom-call | tf_op jit(solution)/shard_map/sum_rest/pallas_call | solution.py:282
  156.6 1.1 add_add_fusion.refs_0_
  157.7 0.1 collective-permute-start.13
  157.9 6.2 %collective-permute-start.23 = (s16[136,1024]{1,0:T(8,128)(2,1)}, s16[136,1024]{1,0:T(8,128)(2,1)S(1)}, u32[]{:S(2)}, u32[]{:S(2)}) collective-permute-start(s16[136,1024]{1,0:T(8,128)(2,1)} %get-tuple-element.62), channel_id=1, source_target_pairs={{0,8},{16,24},{24,16},{1,9},{17,25},{25,17},{2,10},{18,26},{26,18}... | collective-permute-start | bytes 835592 | tf_op jit(solution)/shard_map/ppermute | solution.py:409
  164.1 1.3 collective-permute-start.24
  165.4 3.9 %collective-permute-start.25 = (s16[136,1024]{1,0:T(8,128)(2,1)}, s16[136,1024]{1,0:T(8,128)(2,1)S(1)}, u32[]{:S(2)}, u32[]{:S(2)}) collective-permute-start(s16[136,1024]{1,0:T(8,128)(2,1)} %get-tuple-element.64), channel_id=1, source_target_pairs={{0,24},{8,16},{16,8},{1,25},{9,17},{17,9},{2,26},{10,18},{18,10},{... | collective-permute-start | bytes 835592 | tf_op jit(solution)/shard_map/ppermute | solution.py:409
  169.3 0.8 copy-done.1
  170.1 30.3 %inverse_factor.1.inverse_ref = f32[512,512]{1,0:T(8,128)} custom-call(s32[6]{0:T(128)} %stack.24.place_ref, f32[512,256]{1,0:T(8,128)} %sum_half.1.refs_0_, f32[512,256]{1,0:T(8,128)} %copy-done.1), custom_call_target="tpu_custom_call" | custom-call | tf_op jit(solution)/shard_map/inverse_factor/pallas_call | solution.py:131
  200.4 0.7 copy-done.21
  201.1 8.2 %rows.1 = (f32[512,1024]{1,0:T(8,128)}, f32[512,512]{1,0:T(8,128)}) custom-call(s32[6]{0:T(128)} %stack.24.place_ref, f32[512,512]{1,0:T(8,128)} %inverse_factor.1.inverse_ref, f32[512,1024]{1,0:T(8,128)} %get-tuple-element.45.panel_ref, s16[544,256]{1,0:T(8,128)(2,1)} %copy-done, s16[544,256]{1,0:T(8,128)(2,1)} %copy-done.21), custom_call_target="tpu_custom_call" | custom-call | tf_op jit(solution)/shard_map/rows/pallas_call | solution.py:282
  209.3 0.7 copy-done.22
  210.0 0.1 copy-done.23
  210.1 0.1 copy-done.24
  210.2 7.5 %update.1 = f32[512,1024]{1,0:T(8,128)} custom-call(s32[6]{0:T(128)} %stack.24.place_ref, f32[512,1024]{1,0:T(8,128)} %get-tuple-element.47.factor_ref, f32[512,512]{1,0:T(8,128)} %get-tuple-element.48.row_ref, f32[128,1024]{1,0:T(8,128)} %get-tuple-element.61.own_ref, s16[136,1024]{1,0:T(8,128)(2,1)} %copy-done.22, s16[136,1024]{1,0:T(8,128)(2,1)} %copy-done.23, ...), custom_call_target="tpu_custom_call" | custom-call | tf_op jit(solution)/shard_map/update/pallas_call | solution.py:282
  (60 shorter events, 0.1 us)
Async XLA Ops:
  6.5 51.0 %all-gather.3.cloned.1.call-start = ((), (), s32[]{:S(2)}) async-start(), calls=%async_computation | async-start | bytes 4718592 | tf_op jit(solution)/shard_map/all_gather | solution.py:330
  74.5 13.2 %collective-permute-start.4 = (s16[136,1024]{1,0:T(8,128)(2,1)}, s16[136,1024]{1,0:T(8,128)(2,1)S(1)}, u32[]{:S(2)}, u32[]{:S(2)}) collective-permute-start(s16[136,1024]{1,0:T(8,128)(2,1)} %get-tuple-element.40), channel_id=1, source_target_pairs={{0,8},{8,0},{16,24},{24,16},{1,9},{9,1},{17,25},{25,17},{2,10},{10... | collective-permute-start | bytes 835592 | tf_op jit(solution)/shard_map/ppermute | solution.py:316
  75.7 22.1 %collective-permute-start.5 = (s16[136,1024]{1,0:T(8,128)(2,1)}, s16[136,1024]{1,0:T(8,128)(2,1)S(1)}, u32[]{:S(2)}, u32[]{:S(2)}) collective-permute-start(s16[136,1024]{1,0:T(8,128)(2,1)} %get-tuple-element.41), channel_id=1, source_target_pairs={{0,16},{8,24},{16,0},{24,8},{1,17},{9,25},{17,1},{25,9},{2,18},{10... | collective-permute-start | bytes 835592 | tf_op jit(solution)/shard_map/ppermute | solution.py:316
  75.9 23.2 %collective-permute-start.6 = (s16[136,1024]{1,0:T(8,128)(2,1)}, s16[136,1024]{1,0:T(8,128)(2,1)S(1)}, u32[]{:S(2)}, u32[]{:S(2)}) collective-permute-start(s16[136,1024]{1,0:T(8,128)(2,1)} %get-tuple-element.42), channel_id=1, source_target_pairs={{0,24},{8,16},{16,8},{24,0},{1,25},{9,17},{17,9},{25,1},{2,26},{10... | collective-permute-start | bytes 835592 | tf_op jit(solution)/shard_map/ppermute | solution.py:316
  86.2 16.4 %collective-permute-start.20 = (s16[136,1024]{1,0:T(8,128)(2,1)}, s16[136,1024]{1,0:T(8,128)(2,1)S(1)}, u32[]{:S(2)}, u32[]{:S(2)}) collective-permute-start(s16[136,1024]{1,0:T(8,128)(2,1)} %get-tuple-element.58), channel_id=1, source_target_pairs={{0,8},{8,0},{16,24},{24,16},{1,9},{9,1},{17,25},{25,17},{2,10},{10... | collective-permute-start | bytes 835592 | tf_op jit(solution)/shard_map/ppermute | solution.py:316
  87.4 15.9 %collective-permute-start.21 = (s16[136,1024]{1,0:T(8,128)(2,1)}, s16[136,1024]{1,0:T(8,128)(2,1)S(1)}, u32[]{:S(2)}, u32[]{:S(2)}) collective-permute-start(s16[136,1024]{1,0:T(8,128)(2,1)} %get-tuple-element.59), channel_id=1, source_target_pairs={{0,16},{8,24},{16,0},{24,8},{1,17},{9,25},{17,1},{25,9},{2,18},{10... | collective-permute-start | bytes 835592 | tf_op jit(solution)/shard_map/ppermute | solution.py:316
  87.6 10.2 %copy-start.18 = (s16[136,1024]{1,0:T(8,128)(2,1)}, s16[136,1024]{1,0:T(8,128)(2,1)S(1)}, u32[]{:S(2)}) copy-start(s16[136,1024]{1,0:T(8,128)(2,1)S(1)} %collective-permute-done.4.refs_0_) | copy-start | bytes 835588
  87.6 16.4 %collective-permute-start.22 = (s16[136,1024]{1,0:T(8,128)(2,1)}, s16[136,1024]{1,0:T(8,128)(2,1)S(1)}, u32[]{:S(2)}, u32[]{:S(2)}) collective-permute-start(s16[136,1024]{1,0:T(8,128)(2,1)} %get-tuple-element.60), channel_id=1, source_target_pairs={{0,24},{8,16},{16,8},{24,0},{1,25},{9,17},{17,9},{25,1},{2,26},{10... | collective-permute-start | bytes 835592 | tf_op jit(solution)/shard_map/ppermute | solution.py:316
  97.8 1.5 copy-start.19
  97.8 16.4 %collective-permute-start.17 = (s16[136,1024]{1,0:T(8,128)(2,1)}, s16[136,1024]{1,0:T(8,128)(2,1)S(1)}, u32[]{:S(2)}, u32[]{:S(2)}) collective-permute-start(s16[136,1024]{1,0:T(8,128)(2,1)} %get-tuple-element.54), channel_id=1, source_target_pairs={{0,8},{8,0},{16,24},{24,16},{1,9},{9,1},{17,25},{25,17},{2,10},{10... | collective-permute-start | bytes 835592 | tf_op jit(solution)/shard_map/ppermute | solution.py:316
  99.1 0.7 copy-start.20
  99.1 16.0 %collective-permute-start.18 = (s16[136,1024]{1,0:T(8,128)(2,1)}, s16[136,1024]{1,0:T(8,128)(2,1)S(1)}, u32[]{:S(2)}, u32[]{:S(2)}) collective-permute-start(s16[136,1024]{1,0:T(8,128)(2,1)} %get-tuple-element.55), channel_id=1, source_target_pairs={{0,16},{8,24},{16,0},{24,8},{1,17},{9,25},{17,1},{25,9},{2,18},{10... | collective-permute-start | bytes 835592 | tf_op jit(solution)/shard_map/ppermute | solution.py:316
  102.5 11.7 %copy-start.2 = (s16[136,1024]{1,0:T(8,128)(2,1)}, s16[136,1024]{1,0:T(8,128)(2,1)S(1)}, u32[]{:S(2)}) copy-start(s16[136,1024]{1,0:T(8,128)(2,1)S(1)} %collective-permute-done.20.refs_9_) | copy-start | bytes 835588
  102.5 13.8 %collective-permute-start.9 = (s16[136,1024]{1,0:T(8,128)(2,1)}, s16[136,1024]{1,0:T(8,128)(2,1)S(1)}, u32[]{:S(2)}, u32[]{:S(2)}) collective-permute-start(s16[136,1024]{1,0:T(8,128)(2,1)} %get-tuple-element.44), channel_id=1, source_target_pairs={{0,24},{8,16},{16,8},{24,0},{1,25},{9,17},{17,9},{25,1},{2,26},{10... | collective-permute-start | bytes 835592 | tf_op jit(solution)/shard_map/ppermute | solution.py:316
  103.3 11.0 %copy-start.3 = (s16[136,1024]{1,0:T(8,128)(2,1)}, s16[136,1024]{1,0:T(8,128)(2,1)S(1)}, u32[]{:S(2)}) copy-start(s16[136,1024]{1,0:T(8,128)(2,1)S(1)} %collective-permute-done.21.refs_10_) | copy-start | bytes 835588
  103.3 15.0 %collective-permute-start.8 = (s16[136,1024]{1,0:T(8,128)(2,1)}, s16[136,1024]{1,0:T(8,128)(2,1)S(1)}, u32[]{:S(2)}, u32[]{:S(2)}) collective-permute-start(s16[136,1024]{1,0:T(8,128)(2,1)} %get-tuple-element.44), channel_id=1, source_target_pairs={{0,16},{8,24},{16,0},{24,8},{1,17},{9,25},{17,1},{25,9},{2,18},{10... | collective-permute-start | bytes 835592 | tf_op jit(solution)/shard_map/ppermute | solution.py:316
  104.0 10.2 %copy-start.4 = (s16[136,1024]{1,0:T(8,128)(2,1)}, s16[136,1024]{1,0:T(8,128)(2,1)S(1)}, u32[]{:S(2)}) copy-start(s16[136,1024]{1,0:T(8,128)(2,1)S(1)} %collective-permute-done.22.refs_11_) | copy-start | bytes 835588
  104.0 14.9 %collective-permute-start.7 = (s16[136,1024]{1,0:T(8,128)(2,1)}, s16[136,1024]{1,0:T(8,128)(2,1)S(1)}, u32[]{:S(2)}, u32[]{:S(2)}) collective-permute-start(s16[136,1024]{1,0:T(8,128)(2,1)} %get-tuple-element.44), channel_id=1, source_target_pairs={{0,8},{8,0},{16,24},{24,16},{1,9},{9,1},{17,25},{25,17},{2,10},{10... | collective-permute-start | bytes 835592 | tf_op jit(solution)/shard_map/ppermute | solution.py:316
  105.2 9.1 %copy-start.25 = (s16[136,1024]{1,0:T(8,128)(2,1)S(1)}, s16[136,1024]{1,0:T(8,128)(2,1)}, u32[]{:S(2)}) copy-start(s16[136,1024]{1,0:T(8,128)(2,1)} %get-tuple-element.56) | copy-start | bytes 835588
  114.3 37.0 %copy-start.5 = (s16[136,1024]{1,0:T(8,128)(2,1)}, s16[136,1024]{1,0:T(8,128)(2,1)S(1)}, u32[]{:S(2)}) copy-start(s16[136,1024]{1,0:T(8,128)(2,1)S(1)} %collective-permute-done.17.refs_5_) | copy-start | bytes 835588
  114.3 8.9 %collective-permute-start.19 = (s16[136,1024]{1,0:T(8,128)(2,1)S(1)}, s16[136,1024]{1,0:T(8,128)(2,1)S(1)}, u32[]{:S(2)}, u32[]{:S(2)}) collective-permute-start(s16[136,1024]{1,0:T(8,128)(2,1)S(1)} %copy-done.25), channel_id=1, source_target_pairs={{0,24},{8,16},{16,8},{24,0},{1,25},{9,17},{17,9},{25,1},{2,26},{10... | collective-permute-start | bytes 835592 | tf_op jit(solution)/shard_map/ppermute | solution.py:316
  115.1 36.1 %copy-start.6 = (s16[136,1024]{1,0:T(8,128)(2,1)}, s16[136,1024]{1,0:T(8,128)(2,1)S(1)}, u32[]{:S(2)}) copy-start(s16[136,1024]{1,0:T(8,128)(2,1)S(1)} %collective-permute-done.18.refs_6_) | copy-start | bytes 835588
  115.1 14.1 %collective-permute-start.14 = (s16[136,1024]{1,0:T(8,128)(2,1)}, s16[136,1024]{1,0:T(8,128)(2,1)S(1)}, u32[]{:S(2)}, u32[]{:S(2)}) collective-permute-start(s16[136,1024]{1,0:T(8,128)(2,1)} %get-tuple-element.50), channel_id=1, source_target_pairs={{0,8},{8,0},{16,24},{24,16},{1,9},{9,1},{17,25},{25,17},{2,10},{10... | collective-permute-start | bytes 835592 | tf_op jit(solution)/shard_map/ppermute | solution.py:316
  116.3 3.9 %copy-start.15 = (s16[136,1024]{1,0:T(8,128)(2,1)}, s16[136,1024]{1,0:T(8,128)(2,1)S(1)}, u32[]{:S(2)}) copy-start(s16[136,1024]{1,0:T(8,128)(2,1)S(1)} %collective-permute-done.9.refs_2_) | copy-start | bytes 835588
  116.3 18.8 %collective-permute-start.2 = (s16[544,256]{1,0:T(8,128)(2,1)}, s16[544,256]{1,0:T(8,128)(2,1)S(1)}, u32[]{:S(2)}, u32[]{:S(2)}) collective-permute-start(s16[544,256]{1,0:T(8,128)(2,1)} %get-tuple-element.36), channel_id=1, source_target_pairs={{0,24},{8,16},{16,8},{24,0},{1,25},{9,17},{17,9},{25,1},{2,26},{10... | collective-permute-start | bytes 835592 | tf_op jit(solution)/shard_map/ppermute | solution.py:316
  118.3 1.9 copy-start.16
  118.4 18.9 %collective-permute-start.1 = (s16[544,256]{1,0:T(8,128)(2,1)}, s16[544,256]{1,0:T(8,128)(2,1)S(1)}, u32[]{:S(2)}, u32[]{:S(2)}) collective-permute-start(s16[544,256]{1,0:T(8,128)(2,1)} %get-tuple-element.36), channel_id=1, source_target_pairs={{0,16},{8,24},{16,0},{24,8},{1,17},{9,25},{17,1},{25,9},{2,18},{10... | collective-permute-start | bytes 835592 | tf_op jit(solution)/shard_map/ppermute | solution.py:316
  118.9 1.4 copy-start.17
  118.9 22.3 %collective-permute-start = (s16[544,256]{1,0:T(8,128)(2,1)}, s16[544,256]{1,0:T(8,128)(2,1)S(1)}, u32[]{:S(2)}, u32[]{:S(2)}) collective-permute-start(s16[544,256]{1,0:T(8,128)(2,1)} %get-tuple-element.36), channel_id=1, source_target_pairs={{0,8},{8,0},{16,24},{24,16},{1,9},{9,1},{17,25},{25,17},{2,10},{10... | collective-permute-start | bytes 835592 | tf_op jit(solution)/shard_map/ppermute | solution.py:316
  123.2 28.0 %copy-start.7 = (s16[136,1024]{1,0:T(8,128)(2,1)}, s16[136,1024]{1,0:T(8,128)(2,1)S(1)}, u32[]{:S(2)}) copy-start(s16[136,1024]{1,0:T(8,128)(2,1)S(1)} %collective-permute-done.19.refs_7_) | copy-start | bytes 835588
  123.2 23.1 %collective-permute-start.15 = (s16[136,1024]{1,0:T(8,128)(2,1)}, s16[136,1024]{1,0:T(8,128)(2,1)S(1)}, u32[]{:S(2)}, u32[]{:S(2)}) collective-permute-start(s16[136,1024]{1,0:T(8,128)(2,1)} %get-tuple-element.51), channel_id=1, source_target_pairs={{0,16},{8,24},{16,0},{24,8},{1,17},{9,25},{17,1},{25,9},{2,18},{10... | collective-permute-start | bytes 835592 | tf_op jit(solution)/shard_map/ppermute | solution.py:316
  129.2 22.0 %copy-start.8 = (s16[136,1024]{1,0:T(8,128)(2,1)}, s16[136,1024]{1,0:T(8,128)(2,1)S(1)}, u32[]{:S(2)}) copy-start(s16[136,1024]{1,0:T(8,128)(2,1)S(1)} %collective-permute-done.14.refs_1_) | copy-start | bytes 835588
  129.2 22.0 %collective-permute-start.16 = (s16[136,1024]{1,0:T(8,128)(2,1)}, s16[136,1024]{1,0:T(8,128)(2,1)S(1)}, u32[]{:S(2)}, u32[]{:S(2)}) collective-permute-start(s16[136,1024]{1,0:T(8,128)(2,1)} %get-tuple-element.52), channel_id=1, source_target_pairs={{0,24},{8,16},{16,8},{24,0},{1,25},{9,17},{17,9},{25,1},{2,26},{10... | collective-permute-start | bytes 835592 | tf_op jit(solution)/shard_map/ppermute | solution.py:316
  135.1 9.0 %copy-start.11 = (s16[544,256]{1,0:T(8,128)(2,1)}, s16[544,256]{1,0:T(8,128)(2,1)S(1)}, u32[]{:S(2)}) copy-start(s16[544,256]{1,0:T(8,128)(2,1)S(1)} %collective-permute-done.2.refs_2_) | copy-start | bytes 835588
  135.1 21.5 %collective-permute-start.12 = (s16[544,256]{1,0:T(8,128)(2,1)}, s16[544,256]{1,0:T(8,128)(2,1)S(1)}, u32[]{:S(2)}, u32[]{:S(2)}) collective-permute-start(s16[544,256]{1,0:T(8,128)(2,1)} %get-tuple-element.46), channel_id=1, source_target_pairs={{10,12},{11,13},{20,18},{21,19},{30,24},{31,25}} | collective-permute-start | bytes 835592 | tf_op jit(solution)/shard_map/ppermute | solution.py:396
  137.2 6.8 %copy-start.13 = (s16[544,256]{1,0:T(8,128)(2,1)}, s16[544,256]{1,0:T(8,128)(2,1)S(1)}, u32[]{:S(2)}) copy-start(s16[544,256]{1,0:T(8,128)(2,1)S(1)} %collective-permute-done.1.refs_1_) | copy-start | bytes 835588
  137.2 19.3 %collective-permute-start.11 = (s16[544,256]{1,0:T(8,128)(2,1)}, s16[544,256]{1,0:T(8,128)(2,1)S(1)}, u32[]{:S(2)}, u32[]{:S(2)}) collective-permute-start(s16[544,256]{1,0:T(8,128)(2,1)} %get-tuple-element.46), channel_id=1, source_target_pairs={{10,14},{11,15},{20,16},{21,17},{30,26},{31,27}} | collective-permute-start | bytes 835592 | tf_op jit(solution)/shard_map/ppermute | solution.py:396
  141.2 2.9 %copy-start.14 = (s16[544,256]{1,0:T(8,128)(2,1)}, s16[544,256]{1,0:T(8,128)(2,1)S(1)}, u32[]{:S(2)}) copy-start(s16[544,256]{1,0:T(8,128)(2,1)S(1)} %collective-permute-done.refs_0_) | copy-start | bytes 835588
  141.2 15.4 %collective-permute-start.10 = (s16[544,256]{1,0:T(8,128)(2,1)}, s16[544,256]{1,0:T(8,128)(2,1)}, u32[]{:S(2)}, u32[]{:S(2)}) collective-permute-start(s16[544,256]{1,0:T(8,128)(2,1)} %get-tuple-element.46), channel_id=1, source_target_pairs={{10,8},{11,9},{20,22},{21,23},{30,28},{31,29}} | collective-permute-start | bytes 835592 | tf_op jit(solution)/shard_map/ppermute | solution.py:396
  146.4 10.2 %copy-start.9 = (s16[544,256]{1,0:T(8,128)(2,1)S(1)}, s16[544,256]{1,0:T(8,128)(2,1)}, u32[]{:S(2)}) copy-start(s16[544,256]{1,0:T(8,128)(2,1)} %get-tuple-element.46) | copy-start | bytes 835588
  146.4 4.9 %copy-start.10 = (s16[136,1024]{1,0:T(8,128)(2,1)}, s16[136,1024]{1,0:T(8,128)(2,1)S(1)}, u32[]{:S(2)}) copy-start(s16[136,1024]{1,0:T(8,128)(2,1)S(1)} %collective-permute-done.15.refs_2_) | copy-start | bytes 835588
  146.4 22.9 %collective-permute-start.3 = (f32[512,256]{1,0:T(8,128)}, f32[512,256]{1,0:T(8,128)S(1)}, u32[]{:S(2)}, u32[]{:S(2)}) collective-permute-start(f32[512,256]{1,0:T(8,128)} %sum_half.1.refs_0_), channel_id=1, source_target_pairs={{0,1},{1,0},{2,3},{3,2},{4,5},{5,4},{6,7},{7,6},{8,9},{9,8},{10,11... | collective-permute-start | bytes 1572872 | tf_op jit(solution)/shard_map/ppermute | solution.py:324
  151.3 0.7 copy-start.12
  157.7 42.7 %copy-start = (s16[544,256]{1,0:T(8,128)(2,1)}, s16[544,256]{1,0:T(8,128)(2,1)S(1)}, u32[]{:S(2)}) copy-start(s16[544,256]{1,0:T(8,128)(2,1)S(1)} %add_add_fusion.refs_0_) | copy-start | bytes 835588
  157.7 42.7 %collective-permute-start.13 = (s16[544,256]{1,0:T(8,128)(2,1)S(1)}, s16[544,256]{1,0:T(8,128)(2,1)S(1)}, u32[]{:S(2)}, u32[]{:S(2)}) collective-permute-start(s16[544,256]{1,0:T(8,128)(2,1)S(1)} %add_add_fusion.refs_0_), channel_id=1, source_target_pairs={{0,1},{1,0},{2,3},{3,2},{4,5},{5,4},{6,7},{7,6},{8,9},{9,8},{10,11... | collective-permute-start | bytes 835592 | tf_op jit(solution)/shard_map/ppermute | solution.py:324
  157.9 51.4 %collective-permute-start.23 = (s16[136,1024]{1,0:T(8,128)(2,1)}, s16[136,1024]{1,0:T(8,128)(2,1)S(1)}, u32[]{:S(2)}, u32[]{:S(2)}) collective-permute-start(s16[136,1024]{1,0:T(8,128)(2,1)} %get-tuple-element.62), channel_id=1, source_target_pairs={{0,8},{16,24},{24,16},{1,9},{17,25},{25,17},{2,10},{18,26},{26,18}... | collective-permute-start | bytes 835592 | tf_op jit(solution)/shard_map/ppermute | solution.py:409
  164.1 45.3 %collective-permute-start.24 = (s16[136,1024]{1,0:T(8,128)(2,1)}, s16[136,1024]{1,0:T(8,128)(2,1)S(1)}, u32[]{:S(2)}, u32[]{:S(2)}) collective-permute-start(s16[136,1024]{1,0:T(8,128)(2,1)} %get-tuple-element.63), channel_id=1, source_target_pairs={{0,16},{8,24},{24,8},{1,17},{9,25},{25,9},{2,18},{10,26},{26,10},{... | collective-permute-start | bytes 835592 | tf_op jit(solution)/shard_map/ppermute | solution.py:409
  165.4 44.0 %collective-permute-start.25 = (s16[136,1024]{1,0:T(8,128)(2,1)}, s16[136,1024]{1,0:T(8,128)(2,1)S(1)}, u32[]{:S(2)}, u32[]{:S(2)}) collective-permute-start(s16[136,1024]{1,0:T(8,128)(2,1)} %get-tuple-element.64), channel_id=1, source_target_pairs={{0,24},{8,16},{16,8},{1,25},{9,17},{17,9},{2,26},{10,18},{18,10},{... | collective-permute-start | bytes 835592 | tf_op jit(solution)/shard_map/ppermute | solution.py:409
  169.3 0.8 copy-start.1
  200.4 0.7 copy-start.21
  209.3 0.7 copy-start.22
  209.3 0.8 copy-start.23
  209.3 0.9 copy-start.24
Sparse Core Ops, SparseCore 0:
  10.4 47.0 all-gather.2
